TPU v7x, 32 devices: a whole 2x2x4 slice. The times are simulated.
32 devices in a mesh: ctx: 8 (over z, y), grp: 4 (over x, core).
Axes of the slice: x: 2, y: 2, z: 4, core: 2. Of those that a mesh axis runs over, the one named last changes fastest.
Arguments:
- channels: bfloat16 [4096, 5120], P(('ctx', 'grp')), may hold values from -6 to 6
- gates: bfloat16 [4096, 5120], P(('ctx', 'grp')), may hold values from -6 to 6
- b_proj: bfloat16 [4096, 128], P(('ctx', 'grp')), may hold values from -6 to 6
- c_proj: bfloat16 [4096, 128], P(('ctx', 'grp')), may hold values from -0.5 to 0.5
- step_size: bfloat16 [4096, 80], P(('ctx', 'grp')), may hold values from 0.001 to 1, as said below
- log_decay: bfloat16 [4096, 80], P(('ctx', 'grp')), may hold values from -1 to 0, as said below
- skip_gain: float32 [80], P('grp'), may hold values from 0.5 to 2
- norm_gain: float32 [5120], P('grp'), may hold values from 0.1 to 1.9
- out_weight: bfloat16 [5120, 2560], P('grp'), may hold values from -0.078125 to 0.078125
Outputs:
- layer_out: bfloat16 [4096, 2560], P(('ctx', 'grp'))
Inputs may be any that keep to these rules, and one draw needn't show every extreme that they name: `step_size`: each token's step of each head is positive. `log_decay`: each token's log decay of each head is negative.
All inputs are finite; a program needn't handle non-finite values.
Results may differ from a plain program's by a relative error of at most 0.009.
Values may be sent and summed in bfloat16 or wider, within the bound.
A program may use at most 128 MiB of HBM per device.

v0:
```python
import jax
import jax.numpy as jnp
from jax import lax
from jax.sharding import PartitionSpec as P

HEADS = 80
HD = 64
NSTATE = 128
GROUP = 256


def prefix_2(value, axis, join, neutral):
    count, mine = (lax.axis_size(axis), lax.axis_index(axis))
    pieces = jax.tree.map(lambda part: lax.all_gather(part, axis), value)
    so_far = jax.tree.map(
        lambda part, zero: jnp.full_like(part, 0) + jnp.asarray(zero, part.dtype), value, neutral
    )

    def turn(position, so_far):
        longer = join(so_far, jax.tree.map(lambda part: part[position], pieces))
        return jax.tree.map(lambda new, old: jnp.where(position < mine, new, old), longer, so_far)

    return lax.fori_loop(0, count - 1, turn, so_far)


def local_scan(chan_heads, step_heads, decay_heads, b_rows, c_rows):
    highest = lax.Precision.HIGHEST
    piece_len = chan_heads.shape[0]
    nheads = step_heads.shape[1]
    blocks = piece_len // GROUP
    running = jnp.cumsum(decay_heads.astype(jnp.float32).reshape(blocks, GROUP, nheads), axis=1)
    running_t = jnp.transpose(running, (0, 2, 1))
    chan_f = chan_heads.astype(jnp.float32).reshape(piece_len, nheads, HD)
    inputs = (chan_f * step_heads.astype(jnp.float32)[:, :, None]).reshape(
        blocks, GROUP, nheads, HD
    )
    b_blocks = b_rows.reshape(blocks, GROUP, NSTATE)
    c_blocks = c_rows.reshape(blocks, GROUP, NSTATE)
    scores = jnp.einsum("qin,qjn->qij", c_blocks, b_blocks, preferred_element_type=jnp.float32)
    rows_at = lax.broadcasted_iota(jnp.int32, (GROUP, GROUP), 0)
    cols_at = lax.broadcasted_iota(jnp.int32, (GROUP, GROUP), 1)
    causal = rows_at >= cols_at
    spread = running_t[:, :, :, None] - running_t[:, :, None, :]
    weights = jnp.where(causal[None, None], jnp.exp(spread), 0.0) * scores[:, None]
    y_intra = jnp.einsum("qhij,qjhp->qihp", weights, inputs, precision=highest)
    tail_decay = jnp.exp(running[:, -1:, :] - running)
    b_float = b_blocks.astype(jnp.float32)
    c_float = c_blocks.astype(jnp.float32)
    group_states = jnp.einsum(
        "qjhp,qjn->qhpn", inputs * tail_decay[..., None], b_float, precision=highest
    )
    totals = jnp.exp(running[:, -1, :])

    def carry_step(carried, packed):
        factor, fresh_state = packed
        return (factor[:, None, None] * carried + fresh_state, carried)

    final_state, starts = lax.scan(
        carry_step, jnp.zeros((nheads, HD, NSTATE), jnp.float32), (totals, group_states)
    )
    y_inter = (
        jnp.einsum("qin,qhpn->qihp", c_float, starts, precision=highest)
        * jnp.exp(running)[..., None]
    )
    group_logs = running[:, -1, :]
    offsets = jnp.cumsum(group_logs, axis=0) - group_logs
    piece_cum = (running + offsets[:, None, :]).reshape(piece_len, nheads)
    piece_log = jnp.sum(group_logs, axis=0)
    local_out = (y_intra + y_inter).reshape(piece_len, nheads, HD)
    return (local_out, final_state, piece_log, piece_cum, chan_f)


def local(channels, gates, b_proj, c_proj, step_size, log_decay, skip_gain, norm_gain, out_weight):
    highest = lax.Precision.HIGHEST
    chan_heads, gate_heads, step_heads, decay_heads = (
        lax.all_to_all(channels, "grp", split_axis=1, concat_axis=0, tiled=True),
        lax.all_to_all(gates, "grp", split_axis=1, concat_axis=0, tiled=True),
        lax.all_to_all(step_size, "grp", split_axis=1, concat_axis=0, tiled=True),
        lax.all_to_all(log_decay, "grp", split_axis=1, concat_axis=0, tiled=True),
    )
    b_rows, c_rows = (
        lax.all_gather(b_proj, "grp", axis=0, tiled=True),
        lax.all_gather(c_proj, "grp", axis=0, tiled=True),
    )
    local_out, final_state, piece_log, piece_cum, chan_f = local_scan(
        chan_heads, step_heads, decay_heads, b_rows, c_rows
    )
    piece_factor = jnp.exp(piece_log)

    def combine(early_part, later_part):
        return (
            early_part[0] * later_part[0],
            later_part[0][:, None, None] * early_part[1] + later_part[1],
        )

    identity = (jnp.ones_like(piece_factor), jnp.zeros_like(final_state))
    prefix = prefix_2((piece_factor, final_state), "ctx", combine, identity)
    incoming = prefix[1]
    correction = jnp.einsum("tn,hpn->thp", c_rows.astype(jnp.float32), incoming, precision=highest)
    correction = correction * jnp.exp(piece_cum)[:, :, None]
    ssm_out = local_out + correction + skip_gain[None, :, None] * chan_f
    piece_len = chan_heads.shape[0]
    gated_out = ssm_out.reshape(piece_len, chan_heads.shape[1]) * jax.nn.silu(
        gate_heads.astype(jnp.float32)
    )
    row_squares = lax.psum(jnp.sum(gated_out * gated_out, axis=1), "grp")
    scale = lax.rsqrt(row_squares / (HEADS * HD) + 1e-05)
    normed = (gated_out * scale[:, None] * norm_gain[None, :]).astype(jnp.bfloat16)
    return lax.psum_scatter(
        jnp.dot(normed, out_weight, preferred_element_type=jnp.float32).astype(jnp.bfloat16),
        "grp",
        scatter_dimension=0,
        tiled=True,
    )


def solution(mesh):
    in_specs = (
        P(("ctx", "grp"), None),
        P(("ctx", "grp"), None),
        P(("ctx", "grp"), None),
        P(("ctx", "grp"), None),
        P(("ctx", "grp"), None),
        P(("ctx", "grp"), None),
        P("grp"),
        P("grp"),
        P("grp", None),
    )
    out_specs = P(("ctx", "grp"), None)
    return jax.shard_map(local, mesh=mesh, in_specs=in_specs, out_specs=out_specs, check_vma=False)
```

profile of v0, /device:TPU:0, one launch (start us, length us, event | category | flops | bytes accessed | tf_op | source)
XLA Modules:
  0.0 233.1 jit_solution(6459703165636211416)
XLA Ops:
  6.5 1.4 all_to_all.44
  7.9 4.2 %all-to-all-start.2 = ((bf16[128,4,20]{0,2,1:T(8,128)(2,1)}), bf16[128,4,20]{0,2,1:T(8,128)(2,1)S(1)}, u32[]{:S(2)}, u32[]{:S(2)}) async-start(bf16[128,4,20]{0,2,1:T(8,128)(2,1)} %all_to_all.44), calls=%async_computation.2 | async-start | bytes 49152 | tf_op jit(solution)/shard_map/all_to_all | solution.py:79
  12.1 5.8 %all_gather.17 = bf16[512,128]{1,0:T(8,128)(2,1)S(1)} all-gather(bf16[128,128]{1,0:T(8,128)(2,1)} %param.15), channel_id=1, replica_groups=mesh['ctx'=8,'grp'=4] {'grp'}, dimensions={0}, use_global_device_ids=true | all-gather | bytes 163840 | tf_op jit(solution)/shard_map/all_gather | solution.py:82
  17.9 2.4 %copy.51 = bf16[128,5120]{0,1:T(8,128)(2,1)} copy(bf16[128,5120]{1,0:T(8,128)(2,1)} %param.13) | data formatting | bytes 2621440 | tf_op args[0]
  20.9 3.3 %all-to-all-start.1 = ((bf16[128,4,20]{0,2,1:T(8,128)(2,1)}), bf16[128,4,20]{0,2,1:T(8,128)(2,1)S(1)}, u32[]{:S(2)}, u32[]{:S(2)}) async-start(bf16[128,4,20]{0,2,1:T(8,128)(2,1)} %all_to_all.42), calls=%async_computation.1 | async-start | bytes 49152 | tf_op jit(solution)/shard_map/all_to_all | solution.py:78
  24.3 1.2 reduce-window.6
  25.7 2.3 %all-to-all-done.1 = bf16[128,4,20]{0,2,1:T(8,128)(2,1)S(1)} async-done(((bf16[128,4,20]{0,2,1:T(8,128)(2,1)}), bf16[128,4,20]{0,2,1:T(8,128)(2,1)S(1)}, u32[]{:S(2)}, u32[]{:S(2)}) %all-to-all-start.1) | async-done | bytes 20512 | tf_op jit(solution)/shard_map/all_to_all | solution.py:78
  28.1 3.5 %all-to-all-start = ((bf16[128,4,1280]{0,2,1:T(8,128)(2,1)}), bf16[128,4,1280]{0,2,1:T(8,128)(2,1)S(1)}, u32[]{:S(2)}, u32[]{:S(2)}) async-start(bf16[128,4,1280]{0,2,1:T(8,128)(2,1)} %bitcast), calls=%async_computation | async-start | bytes 2621440 | tf_op jit(solution)/shard_map/all_to_all | solution.py:76
  33.5 15.3 %all-to-all-done = bf16[128,4,1280]{0,2,1:T(8,128)(2,1)S(1)} async-done(((bf16[128,4,1280]{0,2,1:T(8,128)(2,1)}), bf16[128,4,1280]{0,2,1:T(8,128)(2,1)S(1)}, u32[]{:S(2)}, u32[]{:S(2)}) %all-to-all-start) | async-done | bytes 1310752 | tf_op jit(solution)/shard_map/all_to_all | solution.py:76
  49.0 5.4 %copy.52 = f32[4,128,1280]{1,0,2:T(4,128)S(1)} copy(f32[4,128,1280]{1,2,0:T(8,128)S(1)} %convert_bitcast_fusion.1) | data formatting | bytes 5242880 | tf_op jit(solution)/shard_map/convert_element_type | solution.py:33
  54.5 3.3 %reshape.122 = f32[2,256,20,64]{1,0,3,2:T(2,128)} reshape(f32[4,128,1280]{1,0,2:T(4,128)S(1)} %copy.52) | data formatting | bytes 5242880 | tf_op jit(solution)/shard_map/convert_element_type | solution.py:33
  57.8 5.1 %broadcast_multiply_fusion = (f32[2,256,20,64]{1,0,3,2:T(2,128)S(1)}, f32[2,256,20,64]{1,0,3,2:T(2,128)}) fusion(f32[2,256,20]{1,0,2:T(2,128)S(1)} %get-tuple-element.189, f32[2,256,20,64]{1,0,3,2:T(2,128)} %reshape.122, f32[2,256,20]{1,0,2:T(2,128)S(1)} %reshape.123), kind=kLoop, calls=%fused_computation.39 | loop fusion | flops 1310720 | bytes 7946240 | tf_op jit(solution)/shard_map/mul | solution.py:50
  62.9 2.4 %fusion.22 = f32[2,20,64,128]{3,2,1,0:T(8,128)} fusion(bf16[2,256,128,1]{2,1,3,0:T(8,128)(2,1)S(1)} %bitcast.131, f32[2,256,20,64]{1,0,3,2:T(2,128)S(1)} %get-tuple-element.186), kind=kOutput, calls=%fused_computation.33 | convolution fusion | flops 1006632960 | bytes 4063232 | tf_op jit(solution)/shard_map/qjhp,qjn->qhpn/dot_general | solution.py:49
  65.3 4.3 %while.27 = (s32[]{:T(128)}, f32[20,64,128]{2,1,0:T(8,128)S(1)}, f32[2,20,64,128]{3,2,1,0:T(8,128)}, f32[2,20]{1,0:T(2,128)S(1)}, f32[2,20,64,128]{3,2,1,0:T(8,128)}, /*index=5*/s32[]{:T(128)}, s32[]{:T(128)}) while((s32[]{:T(128)}, f32[20,64,128]{2,1,0:T(8,128)S(1)}, f32[2,20,64,128]{3,2,1,0:T(8,128)}, f32[2,20]{1,0:T(2,128)S(1)}, ...), condition=%wide.region_3.4_spmd.clone, body=%wide.region_2.3_spmd.clone.sunk | while | flops 655363 | bytes 3277648 | solution.py:58
  65.3 0.9 bitcast_dynamic-update-slice_fusion.2
  66.2 1.2 bitcast_add_fusion.3
  67.5 0.9 bitcast_dynamic-update-slice_fusion.2
  68.4 1.2 bitcast_add_fusion.3
  69.6 0.8 copy-done
  70.5 2.5 %copy.68 = bf16[128,5120]{0,1:T(8,128)(2,1)} copy(bf16[128,5120]{1,0:T(8,128)(2,1)} %param.14) | data formatting | bytes 2621440 | tf_op args[1]
  72.9 4.3 %all-to-all-start.3 = ((bf16[128,4,1280]{0,2,1:T(8,128)(2,1)}), bf16[128,4,1280]{0,2,1:T(8,128)(2,1)}, u32[]{:S(2)}, u32[]{:S(2)}) async-start(bf16[128,4,1280]{0,2,1:T(8,128)(2,1)} %bitcast.127), calls=%async_computation.3 | async-start | bytes 2621440 | tf_op jit(solution)/shard_map/all_to_all | solution.py:77
  78.5 17.5 %all_gather.16 = bf16[512,128]{1,0:T(8,128)(2,1)S(1)} all-gather(bf16[128,128]{1,0:T(8,128)(2,1)} %param.16), channel_id=1, replica_groups=mesh['ctx'=8,'grp'=4] {'grp'}, dimensions={0}, use_global_device_ids=true | all-gather | bytes 163840 | tf_op jit(solution)/shard_map/all_gather | solution.py:83
  96.7 1.0 fusion.28
  97.7 1.4 copy.57
  100.0 22.7 %all-reduce = f32[160]{0:T(256)S(1)} all-reduce(f32[160]{0:T(256)S(1)} %exponential_dynamic-update-slice_fusion), channel_id=2, replica_groups=mesh['ctx'=8,'grp'=4] {'ctx'}, use_global_device_ids=true, to_apply=%add | all-reduce | flops 160 | bytes 1280
  124.2 2.1 reshape.125
  126.3 13.1 %fusion.2 = f32[2,20,64,256]{3,2,1,0:T(8,128)S(1)} fusion(f32[2,256,256]{2,1,0:T(8,128)} %fusion.28, f32[2,20,256]{2,1,0:T(8,128)} %copy.57, pred[256,256]{1,0:T(8,128)(4,1)S(1)} %copy-done.3, f32[2,256,20,64]{1,0,3,2:T(2,128)} %get-tuple-element.187), kind=kOutput, calls=%fused_computation.7 | convolution fusion | flops 2021130240 | bytes 5873664 | tf_op jit(solution)/shard_map/qhij,qjhp->qihp/dot_general | solution.py:45
  139.5 1.3 fusion.21
  140.9 1.9 copy.74
  142.7 1.6 copy.69
  144.3 1.7 convert_bitcast_fusion
  146.1 4.1 %copy.71 = f32[4,128,1280]{1,0,2:T(4,128)} copy(f32[4,128,1280]{2,1,0:T(8,128)} %convert_bitcast_fusion) | data formatting | bytes 5242880 | tf_op jit(solution)/shard_map/convert_element_type | solution.py:104
  150.2 4.1 %reshape.127 = f32[512,20,64]{0,2,1:T(8,128)} reshape(f32[4,128,1280]{1,0,2:T(4,128)} %copy.71) | data formatting | bytes 5242880 | tf_op jit(solution)/shard_map/convert_element_type | solution.py:104
  154.4 3.5 %all-gather.4.cloned.1.call-done = f32[160,64,128]{2,1,0:T(8,128)} async-done(((f32[20,64,128]{2,1,0:T(8,128)}), f32[160,64,128]{2,1,0:T(8,128)}) %all-gather.4.cloned.1.call-update) | async-done | bytes 5242896 | tf_op jit(solution)/shard_map/all_gather | solution.py:14
  157.9 8.9 %while.28 = (s32[]{:T(128)}, f32[20,64,128]{2,1,0:T(8,128)S(1)}, s32[]{:T(128)}, f32[8,20]{1,0:T(8,128)S(1)}, f32[8,20,64,128]{3,2,1,0:T(8,128)}, /*index=5*/s32[]{:T(128)}, s32[]{:T(128)}) while((s32[]{:T(128)}, f32[20,64,128]{2,1,0:T(8,128)S(1)}, s32[]{:T(128)}, f32[8,20]{1,0:T(8,128)S(1)}, f32[8,20,64,128]{3,2,1,0:T(8,128)}, ...), condition=%wide.region_6.7_spmd.clone, body=%wide.region_5.6_spmd.clone.sunk | while | flops 655364 | bytes 1966425 | solution.py:23
  157.9 1.2 fusion.40
  159.2 1.2 fusion.40
  160.5 1.2 fusion.40
  161.7 1.2 fusion.40
  163.0 1.2 fusion.40
  164.3 1.2 fusion.40
  165.6 1.2 fusion.40
  166.8 6.9 %multiply_reduce_fusion = (f32[512]{0:T(512)S(1)}, f32[512,20,64]{0,2,1:T(8,128)}) fusion(f32[512,20,64]{0,2,1:T(8,128)} %reshape.127, f32[512,20,64]{0,2,1:T(8,128)} %reshape.125, f32[20]{0:T(128)S(1)} %copy-done.7, f32[512,20,64]{0,2,1:T(8,128)} %bitcast.128, f32[512,20]{0,1:T(8,128)S(1)} %bitcast.139, f32[20,64,128]{2,1,0:T(8,128)S(1)} %get-tuple-element.129, ...), kind=kOutput, calls=%fused_computation.37 | convolution fusion | flops 1013841408 | bytes 11315280 | tf_op jit(solution)/shard_map/tn,hpn->thp/dot_general | solution.py:99
  173.7 3.2 %copy.70 = f32[512,1280]{1,0:T(8,128)} copy(f32[512,1280]{0,1:T(8,128)} %bitcast.129) | data formatting | bytes 5242880 | tf_op jit(solution)/shard_map/reshape | solution.py:103
  176.9 5.9 %psum.7 = f32[512]{0:T(512)S(1)} all-reduce(f32[512]{0:T(512)S(1)} %get-tuple-element.193), channel_id=1, replica_groups=mesh['ctx'=8,'grp'=4] {'grp'}, use_global_device_ids=true, to_apply=%region_9.10 | all-reduce | flops 512 | bytes 4096 | tf_op jit(solution)/shard_map/psum | solution.py:106
  182.9 2.6 %fusion.25 = bf16[512,1280]{1,0:T(8,128)(2,1)S(1)} fusion(f32[512,1280]{1,0:T(8,128)} %copy.70, bf16[128,4,1280]{2,0,1:T(8,128)(2,1)S(1)} %copy.69, f32[1280]{0:T(1024)S(1)} %copy-done.6, f32[512]{0:T(512)S(1)} %add_rsqrt_fusion), kind=kLoop, calls=%fused_computation.38 | loop fusion | flops 5898240 | bytes 5250048 | tf_op jit(solution)/shard_map/convert_element_type | solution.py:108
  185.5 7.7 %convolution_convert_fusion = bf16[512,2560]{1,0:T(8,128)(2,1)} fusion(bf16[512,1280]{1,0:T(8,128)(2,1)S(1)} %fusion.25, bf16[1280,2560]{1,0:T(8,128)(2,1)} %param.21), kind=kOutput, calls=%fused_computation.17 | convolution fusion | flops 3356753920 | bytes 10485760 | tf_op jit(solution)/shard_map/dot_general | solution.py:110
  193.2 33.1 %reduce-scatter.2.cloned.1.call-done = bf16[128,2560]{1,0:T(8,128)(2,1)} async-done(((bf16[512,2560]{1,0:T(8,128)(2,1)}), bf16[128,2560]{1,0:T(8,128)(2,1)}) %reduce-scatter.2.cloned.1.call-update) | async-done | bytes 655376 | tf_op jit(solution)/shard_map/reduce_scatter | solution.py:109
  (69 shorter events, 6.7 us)
Async XLA Ops:
  6.5 13.8 %copy-start.5 = (bf16[128,80]{0,1:T(8,128)(2,1)S(1)}, bf16[128,80]{0,1:T(8,128)(2,1)}, u32[]{:S(2)}) copy-start(bf16[128,80]{0,1:T(8,128)(2,1)} %param.17) | copy-start | bytes 61444
  7.9 13.0 %all-to-all-start.2 = ((bf16[128,4,20]{0,2,1:T(8,128)(2,1)}), bf16[128,4,20]{0,2,1:T(8,128)(2,1)S(1)}, u32[]{:S(2)}, u32[]{:S(2)}) async-start(bf16[128,4,20]{0,2,1:T(8,128)(2,1)} %all_to_all.44), calls=%async_computation.2 | async-start | bytes 49152 | tf_op jit(solution)/shard_map/all_to_all | solution.py:79
  20.9 7.1 %all-to-all-start.1 = ((bf16[128,4,20]{0,2,1:T(8,128)(2,1)}), bf16[128,4,20]{0,2,1:T(8,128)(2,1)S(1)}, u32[]{:S(2)}, u32[]{:S(2)}) async-start(bf16[128,4,20]{0,2,1:T(8,128)(2,1)} %all_to_all.42), calls=%async_computation.1 | async-start | bytes 49152 | tf_op jit(solution)/shard_map/all_to_all | solution.py:78
  28.1 20.8 %all-to-all-start = ((bf16[128,4,1280]{0,2,1:T(8,128)(2,1)}), bf16[128,4,1280]{0,2,1:T(8,128)(2,1)S(1)}, u32[]{:S(2)}, u32[]{:S(2)}) async-start(bf16[128,4,1280]{0,2,1:T(8,128)(2,1)} %bitcast), calls=%async_computation | async-start | bytes 2621440 | tf_op jit(solution)/shard_map/all_to_all | solution.py:76
  31.6 126.3 %all-gather.4.cloned.1.call-start = ((), (), s32[]{:S(2)}) async-start(), calls=%async_computation.6 | async-start | bytes 5898240 | tf_op jit(solution)/shard_map/all_gather | solution.py:14
  31.8 17.0 %copy-start.2 = (f32[2,20,256]{2,0,1:T(2,128)}, f32[2,20,256]{2,0,1:T(2,128)S(1)}, u32[]{:S(2)}) copy-start(f32[2,20,256]{2,0,1:T(2,128)S(1)} %reduce_window_sum.35) | copy-start | bytes 122884
  69.6 0.8 copy-start
  70.5 6.9 %copy-start.8 = (u32[32]{0:T(128)S(1)}, u32[32]{0:T(128)}, u32[]{:S(2)}) copy-start(u32[32]{0:T(128)} %constant.61) | copy-start | bytes 388
  72.9 69.8 %all-to-all-start.3 = ((bf16[128,4,1280]{0,2,1:T(8,128)(2,1)}), bf16[128,4,1280]{0,2,1:T(8,128)(2,1)}, u32[]{:S(2)}, u32[]{:S(2)}) async-start(bf16[128,4,1280]{0,2,1:T(8,128)(2,1)} %bitcast.127), calls=%async_computation.3 | async-start | bytes 2621440 | tf_op jit(solution)/shard_map/all_to_all | solution.py:77
  77.3 149.0 %reduce-scatter.2.cloned.1.call-start = ((), (), s32[]{:S(2)}) async-start(), calls=%async_computation.5 | async-start | bytes 3276800 | tf_op jit(solution)/shard_map/reduce_scatter | solution.py:109
  124.2 2.1 copy-start.3
  126.3 13.1 %copy-start.1 = (f32[2,20,64,128]{3,2,1,0:T(8,128)S(1)}, f32[2,20,64,128]{3,2,1,0:T(8,128)}, u32[]{:S(2)}) copy-start(f32[2,20,64,128]{3,2,1,0:T(8,128)} %get-tuple-element.127) | copy-start | bytes 3932164
  157.9 8.9 %copy-start.4 = (f32[3,8,2,256]{3,1,2,0:T(8,128)S(1)}, f32[3,8,2,256]{3,1,2,0:T(8,128)}, u32[]{:S(2)}) copy-start(f32[3,8,2,256]{3,1,2,0:T(8,128)} %copy.75) | copy-start | bytes 147460
  157.9 8.9 %copy-start.7 = (f32[20]{0:T(128)S(1)}, f32[20]{0:T(128)}, u32[]{:S(2)}) copy-start(f32[20]{0:T(128)} %param.19) | copy-start | bytes 244
  173.7 9.2 %copy-start.6 = (f32[1280]{0:T(1024)S(1)}, f32[1280]{0:T(1024)}, u32[]{:S(2)}) copy-start(f32[1280]{0:T(1024)} %param.20) | copy-start | bytes 15364
Sparse Core Ops, SparseCore 0:
  70.6 87.2 all-gather.3
  193.3 32.9 reduce-scatter.1
where the time goes:
time: 235 us; the launch traced here: 233 us
  waiting for transfers between devices  54.3 us (23%)
  blocking collectives  51.9 us (22%)
  local copies, waits for them, and re-layouts  38.9 us (17%)
  matrix products  32.5 us (14%)
  other arithmetic  25.6 us (11%)
  starting transfers between devices  15.4 us (7%)
  between operations  14.3 us (6%)
    reduce_scatter x1, waiting for transfers between devices, local(): lax.psum_scatter(jnp.dot(normed, out_weight, preferred_element_type=jnp.f...  33.1 us
    unnamed x1, blocking collectives  22.7 us
    all_gather x1, blocking collectives, local(): lax.all_gather(c_proj, 'grp', axis=0, tiled=True)  17.5 us
    all_to_all x1, waiting for transfers between devices, local(): lax.all_to_all(channels, 'grp', split_axis=1, concat_axis=0, tiled=True)  15.3 us
    dot_general x1, matrix products, local_scan(): y_intra = jnp.einsum('qhij,qjhp->qihp', weights, inputs, precision=highest)  13.1 us
    convert_element_type x3, local copies, waits for them, and re-layouts, local_scan(): chan_f = chan_heads.astype(jnp.float32).reshape(piece_len, nheads, HD)  10.9 us
    select_n x7, other arithmetic, turn(): jnp.where(position < mine, new, old)  8.64 us
    convert_element_type x2, local copies, waits for them, and re-layouts, local(): gate_heads.astype(jnp.float32)  8.27 us
  transfers between devices with their start and end apart: 6, of which 4 were waited for; matrix products, arithmetic and copies ran while one was open for 19% of the time, Pallas kernels for 0%

commit v1 on v0

--- a/solution.py
+++ b/solution.py
@@ -103,7 +103,9 @@
     gated_out = ssm_out.reshape(piece_len, chan_heads.shape[1]) * jax.nn.silu(
         gate_heads.astype(jnp.float32)
     )
-    row_squares = lax.psum(jnp.sum(gated_out * gated_out, axis=1), "grp")
+    x = jnp.sum(gated_out * gated_out, axis=1)
+    parts = lax.all_gather(x, "grp")
+    row_squares = jnp.sum(parts, axis=0)
     scale = lax.rsqrt(row_squares / (HEADS * HD) + 1e-05)
     normed = (gated_out * scale[:, None] * norm_gain[None, :]).astype(jnp.bfloat16)
     return lax.psum_scatter(

time: 235 us -> 234 us (level)
    psum x1 -> x0, blocking collectives: 5.91 us -> none  [local(): row_squares = lax.psum(jnp.sum(gated_out * gated_out, axis=1), 'grp')]
    all_gather x0 -> x1, blocking collectives: none -> 5.37 us  [local(): parts = lax.all_gather(x, 'grp')]
where the time goes in v1:
time: 234 us; the launch traced here: 233 us
  waiting for transfers between devices  54.3 us (23%)
  blocking collectives  51.4 us (22%)
  local copies, waits for them, and re-layouts  38.9 us (17%)
  matrix products  32.5 us (14%)
  other arithmetic  25.6 us (11%)
  starting transfers between devices  15.4 us (7%)
  between operations  14.3 us (6%)
    reduce_scatter x1, waiting for transfers between devices, local(): lax.psum_scatter(jnp.dot(normed, out_weight, preferred_element_type=jnp.f...  33 us
    unnamed x1, blocking collectives  22.7 us
    all_gather x1, blocking collectives, local(): lax.all_gather(c_proj, 'grp', axis=0, tiled=True)  17.5 us
    all_to_all x1, waiting for transfers between devices, local(): lax.all_to_all(channels, 'grp', split_axis=1, concat_axis=0, tiled=True)  15.3 us
    dot_general x1, matrix products, local_scan(): y_intra = jnp.einsum('qhij,qjhp->qihp', weights, inputs, precision=highest)  13.1 us
    convert_element_type x3, local copies, waits for them, and re-layouts, local_scan(): chan_f = chan_heads.astype(jnp.float32).reshape(piece_len, nheads, HD)  10.9 us
    select_n x7, other arithmetic, turn(): jnp.where(position < mine, new, old)  8.64 us
    convert_element_type x2, local copies, waits for them, and re-layouts, local(): gate_heads.astype(jnp.float32)  8.27 us
  transfers between devices with their start and end apart: 6, of which 4 were waited for; matrix products, arithmetic and copies ran while one was open for 19% of the time, Pallas kernels for 0%

profile of v1, /device:TPU:0, one launch (start us, length us, event | category | flops | bytes accessed | tf_op | source)
XLA Modules:
  0.0 232.6 jit_solution(11473839349569721858)
XLA Ops:
  6.5 1.4 all_to_all.44
  7.9 4.2 %all-to-all-start.2 = ((bf16[128,4,20]{0,2,1:T(8,128)(2,1)}), bf16[128,4,20]{0,2,1:T(8,128)(2,1)S(1)}, u32[]{:S(2)}, u32[]{:S(2)}) async-start(bf16[128,4,20]{0,2,1:T(8,128)(2,1)} %all_to_all.44), calls=%async_computation.2 | async-start | bytes 49152 | tf_op jit(solution)/shard_map/all_to_all | solution.py:79
  12.1 5.8 %all_gather.23 = bf16[512,128]{1,0:T(8,128)(2,1)S(1)} all-gather(bf16[128,128]{1,0:T(8,128)(2,1)} %param.15), channel_id=1, replica_groups=mesh['ctx'=8,'grp'=4] {'grp'}, dimensions={0}, use_global_device_ids=true | all-gather | bytes 163840 | tf_op jit(solution)/shard_map/all_gather | solution.py:82
  17.9 2.4 %copy.51 = bf16[128,5120]{0,1:T(8,128)(2,1)} copy(bf16[128,5120]{1,0:T(8,128)(2,1)} %param.13) | data formatting | bytes 2621440 | tf_op args[0]
  20.9 3.3 %all-to-all-start.1 = ((bf16[128,4,20]{0,2,1:T(8,128)(2,1)}), bf16[128,4,20]{0,2,1:T(8,128)(2,1)S(1)}, u32[]{:S(2)}, u32[]{:S(2)}) async-start(bf16[128,4,20]{0,2,1:T(8,128)(2,1)} %all_to_all.42), calls=%async_computation.1 | async-start | bytes 49152 | tf_op jit(solution)/shard_map/all_to_all | solution.py:78
  24.3 1.2 reduce-window.6
  25.7 2.3 %all-to-all-done.1 = bf16[128,4,20]{0,2,1:T(8,128)(2,1)S(1)} async-done(((bf16[128,4,20]{0,2,1:T(8,128)(2,1)}), bf16[128,4,20]{0,2,1:T(8,128)(2,1)S(1)}, u32[]{:S(2)}, u32[]{:S(2)}) %all-to-all-start.1) | async-done | bytes 20512 | tf_op jit(solution)/shard_map/all_to_all | solution.py:78
  28.1 3.5 %all-to-all-start = ((bf16[128,4,1280]{0,2,1:T(8,128)(2,1)}), bf16[128,4,1280]{0,2,1:T(8,128)(2,1)S(1)}, u32[]{:S(2)}, u32[]{:S(2)}) async-start(bf16[128,4,1280]{0,2,1:T(8,128)(2,1)} %bitcast), calls=%async_computation | async-start | bytes 2621440 | tf_op jit(solution)/shard_map/all_to_all | solution.py:76
  33.5 15.3 %all-to-all-done = bf16[128,4,1280]{0,2,1:T(8,128)(2,1)S(1)} async-done(((bf16[128,4,1280]{0,2,1:T(8,128)(2,1)}), bf16[128,4,1280]{0,2,1:T(8,128)(2,1)S(1)}, u32[]{:S(2)}, u32[]{:S(2)}) %all-to-all-start) | async-done | bytes 1310752 | tf_op jit(solution)/shard_map/all_to_all | solution.py:76
  49.0 5.4 %copy.52 = f32[4,128,1280]{1,0,2:T(4,128)S(1)} copy(f32[4,128,1280]{1,2,0:T(8,128)S(1)} %convert_bitcast_fusion.1) | data formatting | bytes 5242880 | tf_op jit(solution)/shard_map/convert_element_type | solution.py:33
  54.5 3.3 %reshape.126 = f32[2,256,20,64]{1,0,3,2:T(2,128)} reshape(f32[4,128,1280]{1,0,2:T(4,128)S(1)} %copy.52) | data formatting | bytes 5242880 | tf_op jit(solution)/shard_map/convert_element_type | solution.py:33
  57.8 5.1 %broadcast_multiply_fusion = (f32[2,256,20,64]{1,0,3,2:T(2,128)S(1)}, f32[2,256,20,64]{1,0,3,2:T(2,128)}) fusion(f32[2,256,20]{1,0,2:T(2,128)S(1)} %get-tuple-element.189, f32[2,256,20,64]{1,0,3,2:T(2,128)} %reshape.126, f32[2,256,20]{1,0,2:T(2,128)S(1)} %reshape.127), kind=kLoop, calls=%fused_computation.39 | loop fusion | flops 1310720 | bytes 7946240 | tf_op jit(solution)/shard_map/mul | solution.py:50
  62.9 2.4 %fusion.22 = f32[2,20,64,128]{3,2,1,0:T(8,128)} fusion(bf16[2,256,128,1]{2,1,3,0:T(8,128)(2,1)S(1)} %bitcast.132, f32[2,256,20,64]{1,0,3,2:T(2,128)S(1)} %get-tuple-element.186), kind=kOutput, calls=%fused_computation.33 | convolution fusion | flops 1006632960 | bytes 4063232 | tf_op jit(solution)/shard_map/qjhp,qjn->qhpn/dot_general | solution.py:49
  65.3 4.3 %while.27 = (s32[]{:T(128)}, f32[20,64,128]{2,1,0:T(8,128)S(1)}, f32[2,20,64,128]{3,2,1,0:T(8,128)}, f32[2,20]{1,0:T(2,128)S(1)}, f32[2,20,64,128]{3,2,1,0:T(8,128)}, /*index=5*/s32[]{:T(128)}, s32[]{:T(128)}) while((s32[]{:T(128)}, f32[20,64,128]{2,1,0:T(8,128)S(1)}, f32[2,20,64,128]{3,2,1,0:T(8,128)}, f32[2,20]{1,0:T(2,128)S(1)}, ...), condition=%wide.region_3.4_spmd.clone, body=%wide.region_2.3_spmd.clone.sunk | while | flops 655363 | bytes 3277648 | solution.py:58
  65.3 0.9 bitcast_dynamic-update-slice_fusion.2
  66.2 1.2 bitcast_add_fusion.3
  67.5 0.9 bitcast_dynamic-update-slice_fusion.2
  68.4 1.2 bitcast_add_fusion.3
  69.6 0.8 copy-done
  70.5 2.5 %copy.68 = bf16[128,5120]{0,1:T(8,128)(2,1)} copy(bf16[128,5120]{1,0:T(8,128)(2,1)} %param.14) | data formatting | bytes 2621440 | tf_op args[1]
  72.9 4.3 %all-to-all-start.3 = ((bf16[128,4,1280]{0,2,1:T(8,128)(2,1)}), bf16[128,4,1280]{0,2,1:T(8,128)(2,1)}, u32[]{:S(2)}, u32[]{:S(2)}) async-start(bf16[128,4,1280]{0,2,1:T(8,128)(2,1)} %bitcast.128), calls=%async_computation.3 | async-start | bytes 2621440 | tf_op jit(solution)/shard_map/all_to_all | solution.py:77
  78.5 17.5 %all_gather.22 = bf16[512,128]{1,0:T(8,128)(2,1)S(1)} all-gather(bf16[128,128]{1,0:T(8,128)(2,1)} %param.16), channel_id=1, replica_groups=mesh['ctx'=8,'grp'=4] {'grp'}, dimensions={0}, use_global_device_ids=true | all-gather | bytes 163840 | tf_op jit(solution)/shard_map/all_gather | solution.py:83
  96.7 1.0 fusion.28
  97.7 1.4 copy.57
  100.0 22.7 %all-reduce = f32[160]{0:T(256)S(1)} all-reduce(f32[160]{0:T(256)S(1)} %exponential_dynamic-update-slice_fusion), channel_id=2, replica_groups=mesh['ctx'=8,'grp'=4] {'ctx'}, use_global_device_ids=true, to_apply=%add | all-reduce | flops 160 | bytes 1280
  124.2 2.1 reshape.129
  126.3 13.1 %fusion.2 = f32[2,20,64,256]{3,2,1,0:T(8,128)S(1)} fusion(f32[2,256,256]{2,1,0:T(8,128)} %fusion.28, f32[2,20,256]{2,1,0:T(8,128)} %copy.57, pred[256,256]{1,0:T(8,128)(4,1)S(1)} %copy-done.3, f32[2,256,20,64]{1,0,3,2:T(2,128)} %get-tuple-element.187), kind=kOutput, calls=%fused_computation.7 | convolution fusion | flops 2021130240 | bytes 5873664 | tf_op jit(solution)/shard_map/qhij,qjhp->qihp/dot_general | solution.py:45
  139.5 1.3 fusion.21
  140.9 1.9 copy.74
  142.7 1.6 copy.69
  144.3 1.7 convert_bitcast_fusion
  146.1 4.1 %copy.71 = f32[4,128,1280]{1,0,2:T(4,128)} copy(f32[4,128,1280]{2,1,0:T(8,128)} %convert_bitcast_fusion) | data formatting | bytes 5242880 | tf_op jit(solution)/shard_map/convert_element_type | solution.py:104
  150.2 4.1 %reshape.131 = f32[512,20,64]{0,2,1:T(8,128)} reshape(f32[4,128,1280]{1,0,2:T(4,128)} %copy.71) | data formatting | bytes 5242880 | tf_op jit(solution)/shard_map/convert_element_type | solution.py:104
  154.4 3.5 %all-gather.6.cloned.1.call-done = f32[160,64,128]{2,1,0:T(8,128)} async-done(((f32[20,64,128]{2,1,0:T(8,128)}), f32[160,64,128]{2,1,0:T(8,128)}) %all-gather.6.cloned.1.call-update) | async-done | bytes 5242896 | tf_op jit(solution)/shard_map/all_gather | solution.py:14
  157.9 8.9 %while.28 = (s32[]{:T(128)}, f32[20,64,128]{2,1,0:T(8,128)S(1)}, s32[]{:T(128)}, f32[8,20]{1,0:T(8,128)S(1)}, f32[8,20,64,128]{3,2,1,0:T(8,128)}, /*index=5*/s32[]{:T(128)}, s32[]{:T(128)}) while((s32[]{:T(128)}, f32[20,64,128]{2,1,0:T(8,128)S(1)}, s32[]{:T(128)}, f32[8,20]{1,0:T(8,128)S(1)}, f32[8,20,64,128]{3,2,1,0:T(8,128)}, ...), condition=%wide.region_6.7_spmd.clone, body=%wide.region_5.6_spmd.clone.sunk | while | flops 655364 | bytes 1966425 | solution.py:23
  157.9 1.2 fusion.40
  159.2 1.2 fusion.40
  160.5 1.2 fusion.40
  161.7 1.2 fusion.40
  163.0 1.2 fusion.40
  164.3 1.2 fusion.40
  165.6 1.2 fusion.40
  166.8 6.9 %multiply_reduce_fusion = (f32[512]{0:T(512)S(1)}, f32[512,20,64]{0,2,1:T(8,128)}) fusion(f32[512,20,64]{0,2,1:T(8,128)} %reshape.131, f32[512,20,64]{0,2,1:T(8,128)} %reshape.129, f32[20]{0:T(128)S(1)} %copy-done.7, f32[512,20,64]{0,2,1:T(8,128)} %bitcast.129, f32[512,20]{0,1:T(8,128)S(1)} %bitcast.140, f32[20,64,128]{2,1,0:T(8,128)S(1)} %get-tuple-element.129, ...), kind=kOutput, calls=%fused_computation.37 | convolution fusion | flops 1013841408 | bytes 11315280 | tf_op jit(solution)/shard_map/tn,hpn->thp/dot_general | solution.py:99
  173.7 3.2 %copy.70 = f32[512,1280]{1,0:T(8,128)} copy(f32[512,1280]{0,1:T(8,128)} %bitcast.130) | data formatting | bytes 5242880 | tf_op jit(solution)/shard_map/reshape | solution.py:103
  176.9 5.4 %all-gather.3 = f32[4,1,512]{2,1,0:T(1,128)S(1)} all-gather(f32[1,1,512]{2,1,0:T(1,128)S(1)} %bitcast.143), channel_id=4, replica_groups=mesh['ctx'=8,'grp'=4] {'grp'}, dimensions={0}, use_global_device_ids=true | all-gather | bytes 10240 | tf_op jit(solution)/shard_map/all_gather | solution.py:107
  182.4 2.6 %fusion.25 = bf16[512,1280]{1,0:T(8,128)(2,1)S(1)} fusion(f32[512,1280]{1,0:T(8,128)} %copy.70, bf16[128,4,1280]{2,0,1:T(8,128)(2,1)S(1)} %copy.69, f32[1280]{0:T(1024)S(1)} %copy-done.6, f32[512]{0:T(512)S(1)} %add_rsqrt_fusion), kind=kLoop, calls=%fused_computation.38 | loop fusion | flops 5898240 | bytes 5250048 | tf_op jit(solution)/shard_map/convert_element_type | solution.py:110
  185.0 7.7 %convolution_convert_fusion = bf16[512,2560]{1,0:T(8,128)(2,1)} fusion(bf16[512,1280]{1,0:T(8,128)(2,1)S(1)} %fusion.25, bf16[1280,2560]{1,0:T(8,128)(2,1)} %param.21), kind=kOutput, calls=%fused_computation.17 | convolution fusion | flops 3356753920 | bytes 10485760 | tf_op jit(solution)/shard_map/dot_general | solution.py:112
  192.7 33.0 %reduce-scatter.2.cloned.1.call-done = bf16[128,2560]{1,0:T(8,128)(2,1)} async-done(((bf16[512,2560]{1,0:T(8,128)(2,1)}), bf16[128,2560]{1,0:T(8,128)(2,1)}) %reduce-scatter.2.cloned.1.call-update) | async-done | bytes 655376 | tf_op jit(solution)/shard_map/reduce_scatter | solution.py:111
  (70 shorter events, 6.7 us)
Async XLA Ops:
  6.5 13.8 %copy-start.5 = (bf16[128,80]{0,1:T(8,128)(2,1)S(1)}, bf16[128,80]{0,1:T(8,128)(2,1)}, u32[]{:S(2)}) copy-start(bf16[128,80]{0,1:T(8,128)(2,1)} %param.17) | copy-start | bytes 61444
  7.9 13.0 %all-to-all-start.2 = ((bf16[128,4,20]{0,2,1:T(8,128)(2,1)}), bf16[128,4,20]{0,2,1:T(8,128)(2,1)S(1)}, u32[]{:S(2)}, u32[]{:S(2)}) async-start(bf16[128,4,20]{0,2,1:T(8,128)(2,1)} %all_to_all.44), calls=%async_computation.2 | async-start | bytes 49152 | tf_op jit(solution)/shard_map/all_to_all | solution.py:79
  20.9 7.1 %all-to-all-start.1 = ((bf16[128,4,20]{0,2,1:T(8,128)(2,1)}), bf16[128,4,20]{0,2,1:T(8,128)(2,1)S(1)}, u32[]{:S(2)}, u32[]{:S(2)}) async-start(bf16[128,4,20]{0,2,1:T(8,128)(2,1)} %all_to_all.42), calls=%async_computation.1 | async-start | bytes 49152 | tf_op jit(solution)/shard_map/all_to_all | solution.py:78
  28.1 20.8 %all-to-all-start = ((bf16[128,4,1280]{0,2,1:T(8,128)(2,1)}), bf16[128,4,1280]{0,2,1:T(8,128)(2,1)S(1)}, u32[]{:S(2)}, u32[]{:S(2)}) async-start(bf16[128,4,1280]{0,2,1:T(8,128)(2,1)} %bitcast), calls=%async_computation | async-start | bytes 2621440 | tf_op jit(solution)/shard_map/all_to_all | solution.py:76
  31.6 126.3 %all-gather.6.cloned.1.call-start = ((), (), s32[]{:S(2)}) async-start(), calls=%async_computation.6 | async-start | bytes 5898240 | tf_op jit(solution)/shard_map/all_gather | solution.py:14
  31.8 17.0 %copy-start.2 = (f32[2,20,256]{2,0,1:T(2,128)}, f32[2,20,256]{2,0,1:T(2,128)S(1)}, u32[]{:S(2)}) copy-start(f32[2,20,256]{2,0,1:T(2,128)S(1)} %reduce_window_sum.35) | copy-start | bytes 122884
  69.6 0.8 copy-start
  70.5 6.9 %copy-start.8 = (u32[32]{0:T(128)S(1)}, u32[32]{0:T(128)}, u32[]{:S(2)}) copy-start(u32[32]{0:T(128)} %constant.61) | copy-start | bytes 388
  72.9 69.8 %all-to-all-start.3 = ((bf16[128,4,1280]{0,2,1:T(8,128)(2,1)}), bf16[128,4,1280]{0,2,1:T(8,128)(2,1)}, u32[]{:S(2)}, u32[]{:S(2)}) async-start(bf16[128,4,1280]{0,2,1:T(8,128)(2,1)} %bitcast.128), calls=%async_computation.3 | async-start | bytes 2621440 | tf_op jit(solution)/shard_map/all_to_all | solution.py:77
  77.3 148.5 %reduce-scatter.2.cloned.1.call-start = ((), (), s32[]{:S(2)}) async-start(), calls=%async_computation.5 | async-start | bytes 3276800 | tf_op jit(solution)/shard_map/reduce_scatter | solution.py:111
  124.2 2.1 copy-start.3
  126.3 13.1 %copy-start.1 = (f32[2,20,64,128]{3,2,1,0:T(8,128)S(1)}, f32[2,20,64,128]{3,2,1,0:T(8,128)}, u32[]{:S(2)}) copy-start(f32[2,20,64,128]{3,2,1,0:T(8,128)} %get-tuple-element.127) | copy-start | bytes 3932164
  157.9 8.9 %copy-start.4 = (f32[3,8,2,256]{3,1,2,0:T(8,128)S(1)}, f32[3,8,2,256]{3,1,2,0:T(8,128)}, u32[]{:S(2)}) copy-start(f32[3,8,2,256]{3,1,2,0:T(8,128)} %copy.75) | copy-start | bytes 147460
  157.9 8.9 %copy-start.7 = (f32[20]{0:T(128)S(1)}, f32[20]{0:T(128)}, u32[]{:S(2)}) copy-start(f32[20]{0:T(128)} %param.19) | copy-start | bytes 244
  173.7 8.7 %copy-start.6 = (f32[1280]{0:T(1024)S(1)}, f32[1280]{0:T(1024)}, u32[]{:S(2)}) copy-start(f32[1280]{0:T(1024)} %param.20) | copy-start | bytes 15364
Sparse Core Ops, SparseCore 0:
  70.6 87.2 all-gather.5
  192.8 32.8 reduce-scatter.1
